TPU v7x, 32 devices: a whole 2x2x4 slice. The times are simulated.
32 devices in a mesh: orb: 16 (over z, x, core), aux: 2 (over y).
Axes of the slice: x: 2, y: 2, z: 4, core: 2. Of those that a mesh axis runs over, the one named last changes fastest.
Arguments:
- three_index: float32 [56, 1024, 2048], P(None, 'aux', 'orb'), may hold values from -0.5 to 0.5
- pair_density: float32 [3136, 3136], P('orb'), as said below
- active_orbitals: int32 [56], replicated, may hold values from 200 to 2047, as said below
- screen_mask: int32 [64, 128], P('aux', 'orb'), may hold values from 0 to 1
- one_density: float32 [56, 56], replicated
- inactive_fock: float32 [2048, 256], P('orb'), may hold values from -6 to 6
- active_fock: float32 [2048, 200], P('orb'), may hold values from -6 to 6
Outputs:
- rotation_gradient: float32 [2048, 256], P(('orb', 'aux'))
Inputs may be any that keep to these rules, and one draw needn't show every extreme that they name: `active_orbitals`: 56 distinct orbital indices. pair_density is symmetric: its entry at (tu, vw) equals that at (vw, tu).
All inputs are finite; a program needn't handle non-finite values.
Results may differ from a plain program's by a relative error of at most 0.0001.
Values sent between devices are 32-bit elements; how exact they have to be, the bound alone decides.
No kernel may reach another device: no remote copies, remote signals or barrier semaphores. Data moves between devices by JAX's collectives and lax.ppermute only.
A program may use at most 128 MiB of HBM per device.

v0:
```python
import jax
import jax.numpy as jnp
from jax import lax
from jax.sharding import PartitionSpec as P


def shards(
    three_index, pair_density, active_orbitals, screen_mask, one_density, inactive_fock, active_fock
):
    highest = lax.Precision.HIGHEST
    act_count = three_index.shape[0]
    slab_count = three_index.shape[1]
    row_count = three_index.shape[2]
    inactive_count = active_fock.shape[1]
    orb_position = lax.axis_index("orb")
    kept_mask = jnp.repeat(
        jnp.repeat(screen_mask.astype(jnp.float32), slab_count // screen_mask.shape[0], axis=0),
        row_count // screen_mask.shape[1],
        axis=1,
    )
    screened = three_index * kept_mask[None]
    global_rows = orb_position * row_count + jnp.arange(row_count, dtype=jnp.int32)
    active_pick = (global_rows[:, None] == active_orbitals[None, :]).astype(jnp.float32)
    partial_pairs = jnp.einsum("wPp,pv->Pvw", screened, active_pick, precision=highest).reshape(
        slab_count, act_count * act_count
    )
    pairs = lax.psum(partial_pairs, "orb")
    column_block = jnp.dot(pairs, pair_density.T, precision=highest)
    half = lax.all_gather(column_block, "orb", axis=1, tiled=True)
    q_partial = jnp.einsum(
        "uPp,Ptu->pt", screened, half.reshape(slab_count, act_count, act_count), precision=highest
    )
    occ_index = jnp.concatenate([jnp.arange(inactive_count, dtype=jnp.int32), active_orbitals])
    row_share = row_count // lax.axis_size("aux")
    aux_offset = lax.axis_index("aux") * row_share
    qmatrix = lax.psum(q_partial, "aux")
    inactive_cols = 2.0 * (inactive_fock[:, :inactive_count] + active_fock)
    active_cols = (
        jnp.dot(inactive_fock[:, inactive_count:], one_density, precision=highest) + qmatrix
    )
    fock = jnp.concatenate([inactive_cols, active_cols], axis=1)
    occ_pick = (global_rows[:, None] == occ_index[None, :]).astype(jnp.float32)
    occupied = lax.psum(jnp.dot(occ_pick.T, fock, precision=highest), "orb")
    fock_mine = lax.dynamic_slice_in_dim(fock, aux_offset, row_share, 0)
    pick_mine = lax.dynamic_slice_in_dim(occ_pick, aux_offset, row_share, 0)
    transposed = jnp.dot(pick_mine, occupied.T, precision=highest)
    return 2.0 * (fock_mine - transposed)


def solution(mesh):
    in_specs = (
        P(None, "aux", "orb"),
        P("orb", None),
        P(),
        P("aux", "orb"),
        P(),
        P("orb", None),
        P("orb", None),
    )
    out_specs = P(("orb", "aux"), None)
    return jax.shard_map(shards, mesh=mesh, in_specs=in_specs, out_specs=out_specs, check_vma=False)
```

profile of v0, /device:TPU:1, one launch (start us, length us, event | category | flops | bytes accessed | tf_op | source)
XLA Modules:
  0.0 370.7 jit_solution(4190907556177980599)
XLA Ops:
  6.5 0.0 copy-start
  6.5 0.0 all-reduce.3.cloned.1.call-start
  6.5 0.8 convert_element_type.2
  7.4 0.1 broadcast_in_dim.4
  7.5 0.1 reshape.16
  7.6 0.1 copy.22
  7.8 13.5 %fusion.7 = f32[512,56,56]{0,1,2:T(8,128)S(1)} fusion(f32[56,512,128]{2,1,0:T(8,128)} %param.7, f32[512,128]{1,0:T(8,128)S(1)} %copy.22, s32[128]{0:T(128)S(1)} %iota_add_fusion, s32[56]{0:T(128)} %param.9), kind=kOutput, calls=%fused_computation.7 | convolution fusion | flops 2469927936 | bytes 21365472 | tf_op jit(solution)/shard_map/wPp,pv->Pvw/dot_general | solution.py:24
  21.2 6.4 %copy.23 = f32[512,56,56]{0,2,1:T(8,128)} copy(f32[512,56,56]{0,1,2:T(8,128)S(1)} %fusion.7) | data formatting | bytes 12845056 | tf_op jit(solution)/shard_map/wPp,pv->Pvw/transpose | solution.py:24
  27.6 0.0 all-reduce.3.cloned.1.call-update
  27.6 0.0 copy-start.2
  27.6 0.0 copy-start.4
  27.6 0.0 copy-start.1
  27.7 0.2 all-gather.3.cloned.1.call-start
  27.9 143.9 %all-reduce.3.cloned.1.call-done = f32[512,3136]{0,1:T(8,128)} async-done(((f32[512,3136]{0,1:T(8,128)}), f32[512,3136]{0,1:T(8,128)}) %all-reduce.3.cloned.1.call-update) | async-done | bytes 6422544 | tf_op jit(solution)/shard_map/psum | solution.py:27
  171.8 0.0 copy-done
  171.8 8.6 %convolution_bitcast_fusion = f32[1,196,512]{2,1,0:T(8,128)} fusion(f32[512,3136]{0,1:T(8,128)} %all-reduce.3.cloned.1.call-done, f32[196,3136]{1,0:T(8,128)S(1)} %copy-done), kind=kOutput, calls=%fused_computation.8 | convolution fusion | flops 3776446464 | bytes 9282560 | tf_op jit(solution)/shard_map/dot_general | solution.py:28
  180.4 0.0 all-gather.3.cloned.1.call-update
  180.4 0.0 all-reduce.5.cloned.1.call-start
  180.5 0.0 copy-done.2
  180.5 0.1 copy.21
  180.6 0.0 copy-done.4
  180.6 0.1 pad_add_fusion
  180.7 0.0 copy-done.1
  180.7 63.3 %all-gather.3.cloned.1.call-done = f32[16,196,512]{2,1,0:T(8,128)} async-done(((f32[1,196,512]{2,1,0:T(8,128)}), f32[16,196,512]{2,1,0:T(8,128)}) %all-gather.3.cloned.1.call-update) | async-done | bytes 6422544 | tf_op jit(solution)/shard_map/all_gather | solution.py:29
  244.0 6.1 %reshape.20 = f32[3136,512]{1,0:T(8,128)} reshape(f32[16,196,512]{2,1,0:T(8,128)} %all-gather.3.cloned.1.call-done) | data formatting | bytes 12845056
  250.2 0.0 copy-start.3
  250.2 15.4 %fusion.11 = f32[128,56]{0,1:T(8,128)S(1)} fusion(f32[512,56,56]{0,2,1:T(8,128)} %bitcast.23, f32[56,512,128]{2,1,0:T(8,128)} %param.7, f32[512,128]{1,0:T(8,128)S(1)} %copy.22), kind=kOutput, calls=%fused_computation.11 | convolution fusion | flops 2469920768 | bytes 21393408 | tf_op jit(solution)/shard_map/uPp,Ptu->pt/dot_general | solution.py:30
  265.5 6.3 %psum.22 = f32[128,56]{0,1:T(8,128)S(1)} all-reduce(f32[128,56]{0,1:T(8,128)S(1)} %fusion.11), channel_id=1, replica_groups=mesh['orb'=16,'aux'=2] {'aux'}, use_global_device_ids=true, to_apply=%region_1.0 | all-reduce | flops 7168 | bytes 57344 | tf_op jit(solution)/shard_map/psum | solution.py:36
  271.8 0.0 copy-done.3
  271.8 0.3 convolution_add_fusion
  272.2 0.1 copy.25
  272.3 1.1 fusion.16
  273.4 0.0 all-reduce.5.cloned.1.call-update
  273.4 0.1 broadcast_compare_fusion
  273.5 88.9 %all-reduce.5.cloned.1.call-done = f32[256,256]{1,0:T(8,128)} async-done(((f32[256,256]{1,0:T(8,128)}), f32[256,256]{1,0:T(8,128)}) %all-reduce.5.cloned.1.call-update) | async-done | bytes 262160 | tf_op jit(solution)/shard_map/psum | solution.py:43
  362.3 1.9 fusion.10
  (4 shorter events, 0.0 us)
Async XLA Ops:
  6.5 165.2 %copy-start = (f32[196,3136]{1,0:T(8,128)S(1)}, f32[196,3136]{1,0:T(8,128)}, u32[]{:S(2)}) copy-start(f32[196,3136]{1,0:T(8,128)} %param.8) | copy-start | bytes 7375876
  6.5 165.2 %all-reduce.3.cloned.1.call-start = ((), (), s32[]{:S(2)}) async-start(), calls=%async_computation | async-start | bytes 12845056 | tf_op jit(solution)/shard_map/psum | solution.py:27
  27.6 152.8 %copy-start.2 = (f32[128,200]{0,1:T(8,128)S(1)}, f32[128,200]{0,1:T(8,128)}, u32[]{:S(2)}) copy-start(f32[128,200]{0,1:T(8,128)} %param.13) | copy-start | bytes 307204
  27.6 153.0 %copy-start.4 = (s32[56]{0:T(128)S(1)}, s32[56]{0:T(128)}, u32[]{:S(2)}) copy-start(s32[56]{0:T(128)} %param.9) | copy-start | bytes 676
  27.6 153.0 %copy-start.1 = (f32[128,256]{1,0:T(8,128)S(1)}, f32[128,256]{1,0:T(8,128)}, u32[]{:S(2)}) copy-start(f32[128,256]{1,0:T(8,128)} %param.12) | copy-start | bytes 393220
  27.7 216.4 %all-gather.3.cloned.1.call-start = ((), (), s32[]{:S(2)}) async-start(), calls=%async_computation.2 | async-start | bytes 6963200 | tf_op jit(solution)/shard_map/all_gather | solution.py:29
  180.4 181.9 %all-reduce.5.cloned.1.call-start = ((), (), s32[]{:S(2)}) async-start(), calls=%async_computation.1 | async-start | bytes 524288 | tf_op jit(solution)/shard_map/psum | solution.py:43
  250.2 21.7 %copy-start.3 = (f32[56,56]{1,0:T(8,128)S(1)}, f32[56,56]{1,0:T(8,128)}, u32[]{:S(2)}) copy-start(f32[56,56]{1,0:T(8,128)} %param.11) | copy-start | bytes 37636
Sparse Core Ops, SparseCore 0:
  27.7 143.9 all-reduce.2
  180.5 63.4 all-gather.2
  273.5 88.8 all-reduce.4
where the time goes:
time: 371 us
  waiting for transfers between devices  296 us (80%)
  matrix products  40.7 us (11%)
  between operations  13.2 us (4%)
  local copies, waits for them, and re-layouts  13 us (4%)
  blocking collectives  6.31 us (2%)
    psum x1, waiting for transfers between devices, shards(): pairs = lax.psum(partial_pairs, 'orb')  144 us
    psum x1, waiting for transfers between devices, shards(): occupied = lax.psum(jnp.dot(occ_pick.T, fock, precision=highest), 'orb')  88.9 us
    all_gather x1, waiting for transfers between devices, shards(): half = lax.all_gather(column_block, 'orb', axis=1, tiled=True)  63.3 us
    dot_general x1, matrix products, shards(): jnp.einsum('uPp,Ptu->pt', screened, half.reshape(slab_count, act_count, a...  15.4 us
    dot_general x1, matrix products, shards(): jnp.einsum('wPp,pv->Pvw', screened, active_pick, precision=highest)  13.5 us
    dot_general x1, matrix products, shards(): column_block = jnp.dot(pairs, pair_density.T, precision=highest)  8.61 us
  transfers between devices with their start and end apart: 3, of which 3 were waited for; matrix products, arithmetic and copies ran while one was open for 0% of the time, Pallas kernels for 0%

commit v1 on v0

--- a/solution.py
+++ b/solution.py
@@ -24,7 +24,14 @@
     partial_pairs = jnp.einsum("wPp,pv->Pvw", screened, active_pick, precision=highest).reshape(
         slab_count, act_count * act_count
     )
-    pairs = lax.psum(partial_pairs, "orb")
+    parts_n = lax.axis_size("orb")
+    pairs, lower = (partial_pairs, 0)
+    while 1 << lower < parts_n:
+        aux = lax.ppermute(
+            pairs, axis_name="orb", perm=tuple(((j0, j0 ^ 1 << lower) for j0 in range(parts_n)))
+        )
+        pairs = pairs + aux
+        lower = lower + 1
     column_block = jnp.dot(pairs, pair_density.T, precision=highest)
     half = lax.all_gather(column_block, "orb", axis=1, tiled=True)
     q_partial = jnp.einsum(

time: 371 us -> 804 us (2.17)
  waiting for transfers between devices: 296 us -> 717 us
  other arithmetic: 1.02 us -> 12 us
    ppermute x0 -> x4, waiting for transfers between devices: none -> 563 us  [shards(): lax.ppermute(pairs, axis_name='orb', perm=tuple(((j0, j0 ^ 1 << lower) fo...]
    psum x1 -> x0, waiting for transfers between devices: 144 us -> none  [shards(): pairs = lax.psum(partial_pairs, 'orb')]
    add x0 -> x3, other arithmetic: none -> 11 us  [shards(): pairs = pairs + aux]
  transfers between devices with their start and end apart: 3 -> 6, of which waited for: 3 -> 6; matrix products, arithmetic and copies ran while one was open for 0% -> 0% of each run, Pallas kernels for 0% -> 0%
where the time goes in v1:
time: 804 us
  waiting for transfers between devices  717 us (89%)
  matrix products  38.7 us (5%)
  between operations  13.6 us (2%)
  other arithmetic  12 us (1%)
  local copies, waits for them, and re-layouts  10.4 us (1%)
    ppermute x4, waiting for transfers between devices, shards(): lax.ppermute(pairs, axis_name='orb', perm=tuple(((j0, j0 ^ 1 << lower) fo...  563 us
    psum x1, waiting for transfers between devices, shards(): occupied = lax.psum(jnp.dot(occ_pick.T, fock, precision=highest), 'orb')  88.8 us
    all_gather x1, waiting for transfers between devices, shards(): half = lax.all_gather(column_block, 'orb', axis=1, tiled=True)  64.9 us
  transfers between devices with their start and end apart: 6, of which 6 were waited for; matrix products, arithmetic and copies ran while one was open for 0% of the time, Pallas kernels for 0%

profile of v1, /device:TPU:1, one launch (start us, length us, event | category | flops | bytes accessed | tf_op | source)
XLA Modules:
  0.0 803.5 jit_solution(17214977238317419113)
XLA Ops:
  6.5 0.0 copy-start
  6.5 0.0 all-gather.3.cloned.1.call-start
  6.5 0.8 convert_element_type.2
  7.4 0.1 broadcast_in_dim.4
  7.5 0.1 reshape.16
  7.6 0.1 copy.22
  7.8 13.6 %fusion.9 = f32[512,56,56]{0,1,2:T(8,128)S(1)} fusion(f32[56,512,128]{2,1,0:T(8,128)} %param.7, f32[512,128]{1,0:T(8,128)S(1)} %copy.22, s32[128]{0:T(128)S(1)} %iota_add_fusion, s32[56]{0:T(128)} %param.9), kind=kOutput, calls=%fused_computation.9 | convolution fusion | flops 2469927936 | bytes 21365472 | tf_op jit(solution)/shard_map/wPp,pv->Pvw/dot_general | solution.py:24
  21.4 3.7 copy.23
  25.1 0.1 collective-permute-start
  25.2 10.4 %collective-permute-done = f32[512,3136]{0,1:T(8,128)} collective-permute-done((f32[512,3136]{0,1:T(8,128)S(1)}, f32[512,3136]{0,1:T(8,128)}, u32[]{:S(2)}, u32[]{:S(2)}) %collective-permute-start) | collective-permute-done | bytes 6422560 | tf_op jit(solution)/shard_map/ppermute | solution.py:30
  35.6 3.6 bitcast_add_fusion
  39.3 2.4 collective-permute-start.1
  41.7 138.5 %collective-permute-done.1 = f32[512,3136]{0,1:T(8,128)} collective-permute-done((f32[512,3136]{0,1:T(8,128)S(1)}, f32[512,3136]{0,1:T(8,128)}, u32[]{:S(2)}, u32[]{:S(2)}) %collective-permute-start.1) | collective-permute-done | bytes 6422560 | tf_op jit(solution)/shard_map/ppermute | solution.py:30
  180.2 3.7 add.40
  183.8 1.3 collective-permute-start.2
  185.1 137.8 %collective-permute-done.2 = f32[512,3136]{0,1:T(8,128)} collective-permute-done((f32[512,3136]{0,1:T(8,128)S(1)}, f32[512,3136]{0,1:T(8,128)}, u32[]{:S(2)}, u32[]{:S(2)}) %collective-permute-start.2) | collective-permute-done | bytes 6422560 | tf_op jit(solution)/shard_map/ppermute | solution.py:30
  323.0 3.7 add.41
  326.6 0.0 copy-start.2
  326.7 0.0 copy-start.4
  326.7 0.0 copy-start.1
  326.7 2.0 collective-permute-start.3
  328.7 276.2 %collective-permute-done.3 = f32[512,3136]{0,1:T(8,128)S(1)} collective-permute-done((f32[512,3136]{0,1:T(8,128)S(1)}, f32[512,3136]{0,1:T(8,128)S(1)}, u32[]{:S(2)}, u32[]{:S(2)}) %collective-permute-start.3) | collective-permute-done | bytes 6422560 | tf_op jit(solution)/shard_map/ppermute | solution.py:30
  604.8 0.0 copy-done
  604.9 6.5 fusion.12
  611.3 0.0 all-gather.3.cloned.1.call-update
  611.3 0.0 all-reduce.2.cloned.1.call-start
  611.4 0.0 copy-done.2
  611.4 0.1 copy.21
  611.5 0.0 copy-done.4
  611.5 0.1 pad_add_fusion
  611.6 0.0 copy-done.1
  611.6 64.9 %all-gather.3.cloned.1.call-done = f32[16,196,512]{2,1,0:T(8,128)} async-done(((f32[1,196,512]{2,1,0:T(8,128)}), f32[16,196,512]{2,1,0:T(8,128)}) %all-gather.3.cloned.1.call-update) | async-done | bytes 6422544 | tf_op jit(solution)/shard_map/all_gather | solution.py:36
  676.5 6.1 reshape.20
  682.7 0.0 copy-start.3
  682.7 15.4 %fusion.16 = f32[128,56]{0,1:T(8,128)S(1)} fusion(f32[512,56,56]{0,2,1:T(8,128)} %bitcast.23, f32[56,512,128]{2,1,0:T(8,128)} %param.7, f32[512,128]{1,0:T(8,128)S(1)} %copy.22), kind=kOutput, calls=%fused_computation.13 | convolution fusion | flops 2469920768 | bytes 21393408 | tf_op jit(solution)/shard_map/uPp,Ptu->pt/dot_general | solution.py:37
  698.0 6.3 psum.14
  704.3 0.0 copy-done.3
  704.4 0.3 convolution_add_fusion
  704.7 0.1 copy.25
  704.8 1.1 fusion.21
  705.9 0.0 all-reduce.2.cloned.1.call-update
  705.9 0.1 broadcast_compare_fusion
  706.0 88.8 %all-reduce.2.cloned.1.call-done = f32[256,256]{1,0:T(8,128)} async-done(((f32[256,256]{1,0:T(8,128)}), f32[256,256]{1,0:T(8,128)}) %all-reduce.2.cloned.1.call-update) | async-done | bytes 262160 | tf_op jit(solution)/shard_map/psum | solution.py:50
  794.8 1.9 fusion.15
  (4 shorter events, 0.0 us)
Async XLA Ops:
  6.5 598.3 %copy-start = (f32[196,3136]{1,0:T(8,128)S(1)}, f32[196,3136]{1,0:T(8,128)}, u32[]{:S(2)}) copy-start(f32[196,3136]{1,0:T(8,128)} %param.8) | copy-start | bytes 7375876
  6.5 670.0 %all-gather.3.cloned.1.call-start = ((), (), s32[]{:S(2)}) async-start(), calls=%async_computation.1 | async-start | bytes 6963200 | tf_op jit(solution)/shard_map/all_gather | solution.py:36
  25.1 10.5 %collective-permute-start = (f32[512,3136]{0,1:T(8,128)S(1)}, f32[512,3136]{0,1:T(8,128)}, u32[]{:S(2)}, u32[]{:S(2)}) collective-permute-start(f32[512,3136]{0,1:T(8,128)S(1)} %bitcast.22), channel_id=1, source_target_pairs={{0,2},{2,0},{4,6},{6,4},{8,10},{10,8},{12,14},{14,12},{16,18},{18,... | collective-permute-start | bytes 19267592 | tf_op jit(solution)/shard_map/ppermute | solution.py:30
  39.3 140.9 %collective-permute-start.1 = (f32[512,3136]{0,1:T(8,128)S(1)}, f32[512,3136]{0,1:T(8,128)}, u32[]{:S(2)}, u32[]{:S(2)}) collective-permute-start(f32[512,3136]{0,1:T(8,128)S(1)} %bitcast_add_fusion), channel_id=1, source_target_pairs={{0,4},{2,6},{4,0},{6,2},{8,12},{10,14},{12,8},{14,10},{16,20},{18,... | collective-permute-start | bytes 19267592 | tf_op jit(solution)/shard_map/ppermute | solution.py:30
  183.8 139.1 %collective-permute-start.2 = (f32[512,3136]{0,1:T(8,128)S(1)}, f32[512,3136]{0,1:T(8,128)}, u32[]{:S(2)}, u32[]{:S(2)}) collective-permute-start(f32[512,3136]{0,1:T(8,128)S(1)} %add.40), channel_id=1, source_target_pairs={{0,8},{2,10},{4,12},{6,14},{8,0},{10,2},{12,4},{14,6},{16,24},{18,... | collective-permute-start | bytes 19267592 | tf_op jit(solution)/shard_map/ppermute | solution.py:30
  326.6 284.7 %copy-start.2 = (f32[128,200]{0,1:T(8,128)S(1)}, f32[128,200]{0,1:T(8,128)}, u32[]{:S(2)}) copy-start(f32[128,200]{0,1:T(8,128)} %param.13) | copy-start | bytes 307204
  326.7 284.9 %copy-start.4 = (s32[56]{0:T(128)S(1)}, s32[56]{0:T(128)}, u32[]{:S(2)}) copy-start(s32[56]{0:T(128)} %param.9) | copy-start | bytes 676
  326.7 284.9 %copy-start.1 = (f32[128,256]{1,0:T(8,128)S(1)}, f32[128,256]{1,0:T(8,128)}, u32[]{:S(2)}) copy-start(f32[128,256]{1,0:T(8,128)} %param.12) | copy-start | bytes 393220
  326.7 278.2 %collective-permute-start.3 = (f32[512,3136]{0,1:T(8,128)S(1)}, f32[512,3136]{0,1:T(8,128)S(1)}, u32[]{:S(2)}, u32[]{:S(2)}) collective-permute-start(f32[512,3136]{0,1:T(8,128)S(1)} %add.41), channel_id=1, source_target_pairs={{0,16},{2,18},{4,20},{6,22},{8,24},{10,26},{12,28},{14,30},{16,0},... | collective-permute-start | bytes 19267592 | tf_op jit(solution)/shard_map/ppermute | solution.py:30
  611.3 183.5 %all-reduce.2.cloned.1.call-start = ((), (), s32[]{:S(2)}) async-start(), calls=%async_computation | async-start | bytes 524288 | tf_op jit(solution)/shard_map/psum | solution.py:50
  682.7 21.7 %copy-start.3 = (f32[56,56]{1,0:T(8,128)S(1)}, f32[56,56]{1,0:T(8,128)}, u32[]{:S(2)}) copy-start(f32[56,56]{1,0:T(8,128)} %param.11) | copy-start | bytes 37636
Sparse Core Ops, SparseCore 0:
  611.5 65.0 all-gather.2
  706.0 88.7 all-reduce.1
